TPU v7x, 32 devices: a whole 2x2x4 slice. The times are simulated.
32 devices in a mesh: groups: 2 (over y), seq: 4 (over z), section: 4 (over x, core).
Axes of the slice: x: 2, y: 2, z: 4, core: 2. Of those that a mesh axis runs over, the one named last changes fastest.
Arguments:
- hidden: bfloat16 [4, 32, 3072], P('section', ('groups', 'seq')), parts along dimension 1, may hold values from -6 to 6
- kv_cache: bfloat16 [4, 4, 32, 2, 3072], P('section', None, ('groups', 'seq')), parts along dimension 2, may hold values from -400 to 400
- w_qkv: bfloat16 [4, 3072, 3, 3072], P('section', None, None, 'seq'), may hold values from -0.109375 to 0.109375
- w_out: bfloat16 [4, 3072, 3072], P('section', None, 'seq'), may hold values from -0.109375 to 0.109375
- norm_gain: float32 [4, 2, 128], P('section'), may hold values from 1 to 2
- modulation: float32 [4, 4, 3, 3072], P('section'), may hold values from -5 to 5
- patch_order: int32 [8], P('groups'), parts along dimension 0, may hold values from 0 to 3, each once
- timestep: int32 [8], P('groups'), parts along dimension 0, may hold values from 0 to 3
Outputs:
- next_hidden: bfloat16 [4, 32, 3072], P('section', ('groups', 'seq')), parts along dimension 1
- fresh_kv: bfloat16 [4, 32, 2, 3072], P('section', ('groups', 'seq')), parts along dimension 1
There are 2 independent parts, one for each index of `groups`. A program takes and returns all parts, laid end to end along the dimension named above; an argument that names none is the same for every part. Nothing has to cross between parts.
Inputs may be any that keep to these rules, and one draw needn't show every extreme that they name: `patch_order`: each section holds a different patch.
All inputs are finite; a program needn't handle non-finite values.
Results may differ from a plain program's by a relative error of at most 0.02.
The roundings to bfloat16 on the way count: a program that leaves them out, or rounds other values in their place, can miss the bound.
Values may be sent and summed in bfloat16 or wider, within the bound.
No kernel may reach another device: no remote copies, remote signals or barrier semaphores. Data moves between devices by JAX's collectives and lax.ppermute only.
A program may use at most 64 MiB of HBM per device.

v0:
```python
import math
import jax
import jax.numpy as jnp
from jax import lax
from jax.sharding import PartitionSpec as P


def passed_along(array, axis, by):
    count = lax.axis_size(axis)
    return lax.ppermute(array, axis, [(i, (i + by) % count) for i in range(count)])


def layer_norm(values_in):
    center = values_in - jnp.mean(values_in, axis=-1, keepdims=True)
    spread = jnp.mean(center * center, axis=-1, keepdims=True)
    return center * lax.rsqrt(spread + 1e-06)


def head_norm(values_in, gain):
    square = jnp.mean(values_in * values_in, axis=-1, keepdims=True)
    return values_in * lax.rsqrt(square + 1e-06) * gain


def body(hidden, kv_cache, w_qkv, w_out, norm_gain, modulation, patch_order, timestep):
    section_index = lax.axis_index("section")
    patch_index = lax.dynamic_index_in_dim(patch_order, section_index, 0, keepdims=False)
    step_index = lax.dynamic_index_in_dim(timestep, section_index, 0, keepdims=False)
    modulate = lax.dynamic_index_in_dim(modulation[0], step_index, 0, keepdims=False)
    model_width = hidden.shape[2]
    head_size = norm_gain.shape[2]
    head_count = model_width // head_size
    col_width = w_qkv.shape[3]
    rows_in = hidden[0].astype(jnp.float32)
    own_count = rows_in.shape[0]
    normed = (layer_norm(rows_in) * (1.0 + modulate[1]) + modulate[0]).astype(jnp.bfloat16)
    w_local = w_qkv[0].reshape(model_width, 3 * col_width)
    projected = jnp.dot(
        lax.all_gather(normed, "seq", axis=0, tiled=True),
        w_local,
        preferred_element_type=jnp.float32,
    ).astype(jnp.bfloat16)
    patch_len = projected.shape[0]
    projected = projected.reshape(patch_len, 3, col_width)
    query_cols = lax.all_gather(projected[:, 0], "seq", axis=1, tiled=True)
    kv_rows = lax.all_to_all(projected[:, 1:], "seq", split_axis=0, concat_axis=2, tiled=True)
    queries = head_norm(
        query_cols.astype(jnp.float32).reshape(patch_len, head_count, head_size), norm_gain[0, 0]
    ).astype(jnp.bfloat16)
    key_rows = head_norm(
        kv_rows[:, 0].astype(jnp.float32).reshape(own_count, head_count, head_size), norm_gain[0, 1]
    ).astype(jnp.bfloat16)
    fresh = jnp.stack([key_rows.reshape(own_count, model_width), kv_rows[:, 1]], axis=1)
    zero = jnp.zeros((), jnp.int32)
    local_kv = lax.dynamic_update_slice(kv_cache[0], fresh[None], (patch_index, zero, zero, zero))
    patch_count = local_kv.shape[0]
    local_keys = local_kv[:, :, 0].reshape(patch_count * own_count, head_count, head_size)
    local_values = local_kv[:, :, 1].reshape(patch_count * own_count, head_count, head_size)
    scores = jnp.einsum(
        "thd,shd->hts", queries, local_keys, preferred_element_type=jnp.float32
    ) / math.sqrt(head_size)
    row_top = lax.pmax(jnp.max(scores, axis=-1), "seq")
    weights = jnp.exp(scores - row_top[:, :, None]).astype(jnp.bfloat16)
    denominator = jnp.sum(weights, axis=-1, dtype=jnp.float32).T
    numerator = jnp.einsum(
        "hts,shd->thd", weights, local_values, preferred_element_type=jnp.float32
    ).reshape(patch_len, model_width)
    totals, counts = (
        lax.psum(numerator.astype(jnp.bfloat16), "seq").astype(jnp.float32),
        lax.psum(denominator.astype(jnp.bfloat16), "seq").astype(jnp.float32),
    )
    attention = (totals.reshape(patch_len, head_count, head_size) / counts[:, :, None]).astype(
        jnp.bfloat16
    )
    attention = attention.reshape(patch_len, model_width)
    out_cols = jnp.dot(attention, w_out[0], preferred_element_type=jnp.float32).astype(jnp.bfloat16)
    out_rows = lax.all_to_all(out_cols, "seq", split_axis=0, concat_axis=1, tiled=True)
    block = (rows_in + modulate[2] * out_rows.astype(jnp.float32)).astype(jnp.bfloat16)
    arrived = passed_along(block, "section", 1)
    return (arrived[None], fresh[None])


def solution(mesh):
    return jax.shard_map(
        body,
        mesh=mesh,
        in_specs=(
            P("section", ("groups", "seq"), None),
            P("section", None, ("groups", "seq"), None, None),
            P("section", None, None, "seq"),
            P("section", None, "seq"),
            P("section", None, None),
            P("section", None, None, None),
            P("groups"),
            P("groups"),
        ),
        out_specs=(
            P("section", ("groups", "seq"), None),
            P("section", ("groups", "seq"), None, None),
        ),
        check_vma=False,
    )
```

profile of v0, /device:TPU:0, one launch (start us, length us, event | category | flops | bytes accessed | tf_op | source)
XLA Modules:
  0.0 156.7 jit_solution(8221485039574207923)
XLA Ops:
  7.2 1.2 dynamic_slice.11
  9.7 0.9 convert_reduce_fusion
  10.6 0.9 fusion.15
  12.2 0.9 constant_dynamic-slice_fusion
  13.1 0.8 fusion.21
  13.9 15.1 %all-gather.1 = bf16[4,4,3072]{2,1,0:T(4,128)(2,1)S(1)} all-gather(bf16[1,4,3072]{2,1,0:T(4,128)(2,1)S(1)} %fusion.21), channel_id=1, replica_groups=mesh['groups'=2,'seq'=4,'section'=4] {'seq'}, dimensions={0}, use_global_device_ids=true | all-gather | bytes 122880 | tf_op jit(solution)/shard_map/all_gather | solution.py:38
  29.0 18.6 %copy.27 = bf16[1,3072,3,768]{1,3,2,0:T(8,128)(2,1)} copy(bf16[1,3072,3,768]{3,1,2,0:T(8,128)(2,1)} %param.10) | data formatting | bytes 28311552 | tf_op args[2]
  47.7 0.0 copy-start.2
  47.7 0.0 copy-start.3
  47.7 0.0 copy-start
  47.7 0.0 copy-start.1
  47.7 8.8 %convolution_convert_fusion = bf16[16,2304]{1,0:T(8,128)(2,1)S(1)} fusion(bf16[16,3072]{1,0:T(8,128)(2,1)S(1)} %reshape.88, bf16[3072,2304]{0,1:T(8,128)(2,1)} %bitcast.72), kind=kOutput, calls=%fused_computation.2 | convolution fusion | flops 226529280 | bytes 14327808 | tf_op jit(solution)/shard_map/dot_general | solution.py:37
  56.5 0.1 reshape.77
  56.6 0.7 slice.47
  57.2 4.7 %all-to-all-start = ((bf16[16,2,768]{2,1,0:T(2,128)(2,1)}), bf16[16,2,768]{2,1,0:T(2,128)(2,1)S(1)}, u32[]{:S(2)}, u32[]{:S(2)}) async-start(bf16[16,2,768]{2,1,0:T(2,128)(2,1)} %slice.47), calls=%async_computation | async-start | bytes 98304 | tf_op jit(solution)/shard_map/all_to_all | solution.py:45
  62.0 0.0 all-reduce.2.cloned.1.call-start
  62.0 14.3 %all-gather = bf16[16,1,3072]{2,1,0:T(2,128)(2,1)S(1)} all-gather(bf16[16,1,768]{2,1,0:T(2,128)(2,1)S(1)} %slice.51), channel_id=2, replica_groups=mesh['groups'=2,'seq'=4,'section'=4] {'seq'}, dimensions={2}, use_global_device_ids=true | all-gather | bytes 122880 | tf_op jit(solution)/shard_map/all_gather | solution.py:44
  76.3 0.2 reshape.84
  76.5 0.1 multiply_reduce_fusion
  76.6 0.0 copy-done.2
  76.6 0.1 multiply_convert_fusion
  76.8 0.0 copy-done.3
  76.8 0.6 dynamic_slice.13
  79.3 0.0 all-to-all-done
  79.4 0.1 slice.49
  79.5 0.1 reduce_sum.50
  79.6 0.1 mul.95
  79.7 0.1 multiply_convert_fusion.1
  79.7 0.0 copy-done
  79.8 0.8 constant_dynamic-update-slice_fusion
  80.5 0.9 slice_reduce_fusion.1
  81.4 0.2 fusion.23
  81.6 18.4 %pmax.7 = f32[24,16]{1,0:T(8,128)S(1)} all-reduce(f32[24,16]{1,0:T(8,128)S(1)} %get-tuple-element.11), channel_id=1, replica_groups=mesh['groups'=2,'seq'=4,'section'=4] {'seq'}, use_global_device_ids=true, to_apply=%region_5.6 | all-reduce | flops 384 | bytes 3072 | tf_op jit(solution)/shard_map/pmax | solution.py:61
  100.1 0.2 fusion.2
  100.3 0.6 copy.52
  101.0 0.0 all-reduce.2.cloned.1.call-update
  101.0 0.1 fusion.22
  101.1 0.1 copy.34
  101.2 8.3 %psum.15 = bf16[16,24]{1,0:T(8,128)(2,1)S(1)} all-reduce(bf16[16,24]{1,0:T(8,128)(2,1)S(1)} %bitcast.89), channel_id=1, replica_groups=mesh['groups'=2,'seq'=4,'section'=4] {'seq'}, use_global_device_ids=true, to_apply=%region_8.9 | all-reduce | flops 384 | bytes 1536 | tf_op jit(solution)/shard_map/psum | solution.py:69
  109.5 24.3 %all-reduce.2.cloned.1.call-done = bf16[16,3072]{1,0:T(8,128)(2,1)} async-done(((bf16[16,3072]{1,0:T(8,128)(2,1)}), bf16[16,3072]{1,0:T(8,128)(2,1)}) %all-reduce.2.cloned.1.call-update) | async-done | bytes 98320 | tf_op jit(solution)/shard_map/psum | solution.py:68
  133.8 0.1 div.43
  133.9 3.1 %fusion.3 = bf16[16,768]{1,0:T(8,128)(2,1)S(1)} fusion(bf16[1,3072,768]{2,1,0:T(8,128)(2,1)} %param.11, f32[2,8,24,128]{3,2,1,0:T(8,128)S(1)} %bitcast.76, bf16[16,3072]{1,0:T(8,128)(2,1)} %all-reduce.2.cloned.1.call-done), kind=kOutput, calls=%fused_computation.6 | convolution fusion | flops 75657216 | bytes 5038080 | tf_op jit(solution)/shard_map/dot_general | solution.py:75
  137.1 8.9 %all_to_all.31 = bf16[4,4,768]{2,1,0:T(4,128)(2,1)S(1)} all-to-all(bf16[4,4,768]{2,1,0:T(4,128)(2,1)S(1)} %all_to_all.27), channel_id=1, replica_groups=mesh['groups'=2,'seq'=4,'section'=4] {'seq'}, dimensions={0} | all-to-all | bytes 49152 | tf_op jit(solution)/shard_map/all_to_all | solution.py:76
  145.9 0.0 copy-done.1
  146.0 0.1 collective-permute-start
  146.0 3.2 %collective-permute-done = bf16[4,3072]{1,0:T(4,128)(2,1)S(1)} collective-permute-done((bf16[4,3072]{1,0:T(4,128)(2,1)S(1)}, bf16[4,3072]{1,0:T(4,128)(2,1)S(1)}, u32[]{:S(2)}, u32[]{:S(2)}) %collective-permute-start) | collective-permute-done | bytes 24608 | tf_op jit(solution)/shard_map/ppermute | solution.py:10
  149.3 0.6 copy.58
  (15 shorter events, 0.3 us)
Async XLA Ops:
  47.7 28.9 %copy-start.2 = (f32[1,2,128]{2,1,0:T(2,128)S(1)}, f32[1,2,128]{2,1,0:T(2,128)}, u32[]{:S(2)}) copy-start(f32[1,2,128]{2,1,0:T(2,128)} %param.12) | copy-start | bytes 3076
  47.7 29.1 %copy-start.3 = (s32[4]{0:T(128)S(1)}, s32[4]{0:T(128)}, u32[]{:S(2)}) copy-start(s32[4]{0:T(128)} %param.14) | copy-start | bytes 52
  47.7 32.1 %copy-start = (bf16[1,4,4,2,3072]{4,3,2,1,0:T(2,128)(2,1)S(1)}, bf16[1,4,4,2,3072]{4,3,2,1,0:T(2,128)(2,1)}, u32[]{:S(2)}) copy-start(bf16[1,4,4,2,3072]{4,3,2,1,0:T(2,128)(2,1)} %param.9) | copy-start | bytes 589828
  47.7 98.3 %copy-start.1 = (bf16[1,4,3072]{2,1,0:T(4,128)(2,1)S(1)}, bf16[1,4,3072]{2,1,0:T(4,128)(2,1)}, u32[]{:S(2)}) copy-start(bf16[1,4,3072]{2,1,0:T(4,128)(2,1)} %param.8) | copy-start | bytes 73732
  57.2 22.1 %all-to-all-start = ((bf16[16,2,768]{2,1,0:T(2,128)(2,1)}), bf16[16,2,768]{2,1,0:T(2,128)(2,1)S(1)}, u32[]{:S(2)}, u32[]{:S(2)}) async-start(bf16[16,2,768]{2,1,0:T(2,128)(2,1)} %slice.47), calls=%async_computation | async-start | bytes 98304 | tf_op jit(solution)/shard_map/all_to_all | solution.py:45
  62.0 71.9 %all-reduce.2.cloned.1.call-start = ((), (), s32[]{:S(2)}) async-start(), calls=%async_computation.2 | async-start | bytes 196608 | tf_op jit(solution)/shard_map/psum | solution.py:68
  146.0 3.3 %collective-permute-start = (bf16[4,3072]{1,0:T(4,128)(2,1)S(1)}, bf16[4,3072]{1,0:T(4,128)(2,1)S(1)}, u32[]{:S(2)}, u32[]{:S(2)}) collective-permute-start(bf16[4,3072]{1,0:T(4,128)(2,1)S(1)} %fusion.19), channel_id=1, source_target_pairs={{0,1},{1,2},{2,3},{3,0},{4,5},{5,6},{6,7},{7,4},{8,9},{9,10},{10,1... | collective-permute-start | bytes 73736 | tf_op jit(solution)/shard_map/ppermute | solution.py:10
Sparse Core Ops, SparseCore 0:
  101.1 32.6 all-reduce.1
where the time goes:
time: 158 us; the launch traced here: 157 us
  blocking collectives  65 us (41%)
  waiting for transfers between devices  27.6 us (17%)
  local copies, waits for them, and re-layouts  23.9 us (15%)
  between operations  18.1 us (11%)
  matrix products  12.4 us (8%)
  other arithmetic  5.08 us (3%)
  starting transfers between devices  4.78 us (3%)
    psum x1, waiting for transfers between devices, body(): lax.psum(numerator.astype(jnp.bfloat16), 'seq').astype(jnp.float32)  24.3 us
    unnamed x11, local copies, waits for them, and re-layouts  19.3 us
    pmax x1, blocking collectives, body(): row_top = lax.pmax(jnp.max(scores, axis=-1), 'seq')  18.4 us
    all_gather x1, blocking collectives, body(): lax.all_gather(normed, 'seq', axis=0, tiled=True)  15.1 us
    all_gather x1, blocking collectives, body(): query_cols = lax.all_gather(projected[:, 0], 'seq', axis=1, tiled=True)  14.3 us
    all_to_all x1, blocking collectives, body(): lax.all_to_all(out_cols, 'seq', split_axis=0, concat_axis=1, tiled=True)  8.86 us
    dot_general x1, matrix products, body(): jnp.dot(lax.all_gather(normed, 'seq', axis=0, tiled=True), w_local, prefe...  8.81 us
    psum x1, blocking collectives, body(): lax.psum(denominator.astype(jnp.bfloat16), 'seq').astype(jnp.float32)  8.35 us
  transfers between devices with their start and end apart: 3, of which 2 were waited for; matrix products, arithmetic and copies ran while one was open for 1% of the time, Pallas kernels for 0%

commit v1 on v0

--- a/solution.py
+++ b/solution.py
@@ -65,7 +65,7 @@
         "hts,shd->thd", weights, local_values, preferred_element_type=jnp.float32
     ).reshape(patch_len, model_width)
     totals, counts = (
-        lax.psum(numerator.astype(jnp.bfloat16), "seq").astype(jnp.float32),
+        jnp.sum(lax.all_gather(numerator.astype(jnp.bfloat16), "seq"), axis=0).astype(jnp.float32),
         lax.psum(denominator.astype(jnp.bfloat16), "seq").astype(jnp.float32),
     )
     attention = (totals.reshape(patch_len, head_count, head_size) / counts[:, :, None]).astype(

time: 158 us -> 134 us (0.85)
  waiting for transfers between devices: 27.6 us -> 3.24 us
  blocking collectives: 65 us -> 79.4 us
  between operations: 18.1 us -> 4.77 us
    psum x1 -> x0, waiting for transfers between devices: 24.3 us -> none  [body(): lax.psum(numerator.astype(jnp.bfloat16), 'seq').astype(jnp.float32)]
    all_gather x0 -> x1, blocking collectives: none -> 14.3 us  [body(): lax.all_gather(numerator.astype(jnp.bfloat16), 'seq')]
    unnamed x11 -> x12, local copies, waits for them, and re-layouts: 19.3 us -> 19.3 us
  transfers between devices with their start and end apart: 3 -> 2, of which waited for: 2 -> 1; matrix products, arithmetic and copies ran while one was open for 1% -> 1% of each run, Pallas kernels for 0% -> 0%
where the time goes in v1:
time: 134 us; the launch traced here: 133 us
  blocking collectives  79.4 us (59%)
  local copies, waits for them, and re-layouts  23.3 us (17%)
  matrix products  12.3 us (9%)
  other arithmetic  5.28 us (4%)
  starting transfers between devices  4.78 us (4%)
  between operations  4.77 us (4%)
  waiting for transfers between devices  3.24 us (2%)
    unnamed x12, local copies, waits for them, and re-layouts  19.3 us
    pmax x1, blocking collectives, body(): row_top = lax.pmax(jnp.max(scores, axis=-1), 'seq')  18.4 us
    all_gather x1, blocking collectives, body(): lax.all_gather(normed, 'seq', axis=0, tiled=True)  15.1 us
    all_gather x1, blocking collectives, body(): lax.all_gather(numerator.astype(jnp.bfloat16), 'seq')  14.3 us
    all_gather x1, blocking collectives, body(): query_cols = lax.all_gather(projected[:, 0], 'seq', axis=1, tiled=True)  14.3 us
    all_to_all x1, blocking collectives, body(): lax.all_to_all(out_cols, 'seq', split_axis=0, concat_axis=1, tiled=True)  8.87 us
    dot_general x1, matrix products, body(): jnp.dot(lax.all_gather(normed, 'seq', axis=0, tiled=True), w_local, prefe...  8.81 us
    psum x1, blocking collectives, body(): lax.psum(denominator.astype(jnp.bfloat16), 'seq').astype(jnp.float32)  8.47 us
  transfers between devices with their start and end apart: 2, of which 1 were waited for; matrix products, arithmetic and copies ran while one was open for 1% of the time, Pallas kernels for 0%

profile of v1, /device:TPU:0, one launch (start us, length us, event | category | flops | bytes accessed | tf_op | source)
XLA Modules:
  0.0 133.1 jit_solution(452358716647131610)
XLA Ops:
  0.6 1.2 dynamic_slice.11
  3.2 0.9 convert_reduce_fusion
  4.1 0.9 fusion.16
  5.7 0.9 constant_dynamic-slice_fusion
  6.6 0.8 fusion.22
  7.4 15.1 %all-gather.1 = bf16[4,4,3072]{2,1,0:T(4,128)(2,1)S(1)} all-gather(bf16[1,4,3072]{2,1,0:T(4,128)(2,1)S(1)} %fusion.22), channel_id=1, replica_groups=mesh['groups'=2,'seq'=4,'section'=4] {'seq'}, dimensions={0}, use_global_device_ids=true | all-gather | bytes 122880 | tf_op jit(solution)/shard_map/all_gather | solution.py:38
  22.5 18.6 %copy.27 = bf16[1,3072,3,768]{1,3,2,0:T(8,128)(2,1)} copy(bf16[1,3072,3,768]{3,1,2,0:T(8,128)(2,1)} %param.10) | data formatting | bytes 28311552 | tf_op args[2]
  41.1 0.0 copy-start.2
  41.1 0.0 copy-start.3
  41.1 0.0 copy-start
  41.1 0.0 copy-start.1
  41.1 8.8 %convolution_convert_fusion = bf16[16,2304]{1,0:T(8,128)(2,1)S(1)} fusion(bf16[16,3072]{1,0:T(8,128)(2,1)S(1)} %reshape.113, bf16[3072,2304]{0,1:T(8,128)(2,1)} %bitcast.72), kind=kOutput, calls=%fused_computation.2 | convolution fusion | flops 226529280 | bytes 14327808 | tf_op jit(solution)/shard_map/dot_general | solution.py:37
  50.0 0.1 reshape.101
  50.0 0.7 slice.47
  50.7 4.7 %all-to-all-start = ((bf16[16,2,768]{2,1,0:T(2,128)(2,1)}), bf16[16,2,768]{2,1,0:T(2,128)(2,1)S(1)}, u32[]{:S(2)}, u32[]{:S(2)}) async-start(bf16[16,2,768]{2,1,0:T(2,128)(2,1)} %slice.47), calls=%async_computation | async-start | bytes 98304 | tf_op jit(solution)/shard_map/all_to_all | solution.py:45
  55.5 14.3 %all-gather = bf16[16,1,3072]{2,1,0:T(2,128)(2,1)S(1)} all-gather(bf16[16,1,768]{2,1,0:T(2,128)(2,1)S(1)} %slice.51), channel_id=2, replica_groups=mesh['groups'=2,'seq'=4,'section'=4] {'seq'}, dimensions={2}, use_global_device_ids=true | all-gather | bytes 122880 | tf_op jit(solution)/shard_map/all_gather | solution.py:44
  69.7 0.2 reshape.109
  69.9 0.1 multiply_reduce_fusion
  70.1 0.0 copy-done.2
  70.1 0.1 multiply_convert_fusion
  70.2 0.0 copy-done.3
  70.2 0.6 dynamic_slice.13
  72.8 0.0 all-to-all-done
  72.9 0.1 slice.49
  72.9 0.1 reduce_sum.62
  73.0 0.1 mul.95
  73.1 0.1 multiply_convert_fusion.1
  73.2 0.0 copy-done
  73.2 0.8 constant_dynamic-update-slice_fusion
  74.0 0.9 slice_reduce_fusion
  74.9 0.2 fusion.24
  75.1 18.4 %pmax.7 = f32[24,16]{1,0:T(8,128)S(1)} all-reduce(f32[24,16]{1,0:T(8,128)S(1)} %get-tuple-element.11), channel_id=1, replica_groups=mesh['groups'=2,'seq'=4,'section'=4] {'seq'}, use_global_device_ids=true, to_apply=%region_5.6 | all-reduce | flops 384 | bytes 3072 | tf_op jit(solution)/shard_map/pmax | solution.py:61
  93.6 0.1 fusion.23
  93.6 0.1 copy.34
  93.7 8.5 %psum.7 = bf16[16,24]{1,0:T(8,128)(2,1)S(1)} all-reduce(bf16[16,24]{1,0:T(8,128)(2,1)S(1)} %bitcast.88), channel_id=1, replica_groups=mesh['groups'=2,'seq'=4,'section'=4] {'seq'}, use_global_device_ids=true, to_apply=%region_8.9 | all-reduce | flops 384 | bytes 1536 | tf_op jit(solution)/shard_map/psum | solution.py:69
  102.2 0.2 fusion.2
  102.6 14.3 %all_gather.12 = bf16[4,16,3072]{2,1,0:T(8,128)(2,1)S(1)} all-gather(bf16[1,16,3072]{2,1,0:T(8,128)(2,1)S(1)} %convert_element_type.112), channel_id=1, replica_groups=mesh['groups'=2,'seq'=4,'section'=4] {'seq'}, dimensions={0}, use_global_device_ids=true | all-gather | bytes 491520 | tf_op jit(solution)/shard_map/all_gather | solution.py:68
  116.9 0.1 reduce_sum.64
  117.0 0.1 fusion.6
  117.1 3.1 %fusion.3 = bf16[16,768]{1,0:T(8,128)(2,1)S(1)} fusion(bf16[1,3072,768]{2,1,0:T(8,128)(2,1)} %param.11, bf16[2,8,24,128]{3,2,1,0:T(8,128)(2,1)S(1)} %bitcast.79), kind=kOutput, calls=%fused_computation.6 | convolution fusion | flops 75509760 | bytes 4841472 | tf_op jit(solution)/shard_map/dot_general | solution.py:75
  120.2 8.9 %all_to_all.31 = bf16[4,4,768]{2,1,0:T(4,128)(2,1)S(1)} all-to-all(bf16[4,4,768]{2,1,0:T(4,128)(2,1)S(1)} %all_to_all.27), channel_id=1, replica_groups=mesh['groups'=2,'seq'=4,'section'=4] {'seq'}, dimensions={0} | all-to-all | bytes 49152 | tf_op jit(solution)/shard_map/all_to_all | solution.py:76
  129.1 0.0 copy-done.1
  129.1 0.1 collective-permute-start
  129.2 3.2 %collective-permute-done = bf16[4,3072]{1,0:T(4,128)(2,1)S(1)} collective-permute-done((bf16[4,3072]{1,0:T(4,128)(2,1)S(1)}, bf16[4,3072]{1,0:T(4,128)(2,1)S(1)}, u32[]{:S(2)}, u32[]{:S(2)}) %collective-permute-start) | collective-permute-done | bytes 24608 | tf_op jit(solution)/shard_map/ppermute | solution.py:10
  132.4 0.6 copy.57
  (20 shorter events, 0.4 us)
Async XLA Ops:
  41.1 28.9 %copy-start.2 = (f32[1,2,128]{2,1,0:T(2,128)S(1)}, f32[1,2,128]{2,1,0:T(2,128)}, u32[]{:S(2)}) copy-start(f32[1,2,128]{2,1,0:T(2,128)} %param.12) | copy-start | bytes 3076
  41.1 29.1 %copy-start.3 = (s32[4]{0:T(128)S(1)}, s32[4]{0:T(128)}, u32[]{:S(2)}) copy-start(s32[4]{0:T(128)} %param.14) | copy-start | bytes 52
  41.1 32.1 %copy-start = (bf16[1,4,4,2,3072]{4,3,2,1,0:T(2,128)(2,1)S(1)}, bf16[1,4,4,2,3072]{4,3,2,1,0:T(2,128)(2,1)}, u32[]{:S(2)}) copy-start(bf16[1,4,4,2,3072]{4,3,2,1,0:T(2,128)(2,1)} %param.9) | copy-start | bytes 589828
  41.1 88.0 %copy-start.1 = (bf16[1,4,3072]{2,1,0:T(4,128)(2,1)S(1)}, bf16[1,4,3072]{2,1,0:T(4,128)(2,1)}, u32[]{:S(2)}) copy-start(bf16[1,4,3072]{2,1,0:T(4,128)(2,1)} %param.8) | copy-start | bytes 73732
  50.7 22.1 %all-to-all-start = ((bf16[16,2,768]{2,1,0:T(2,128)(2,1)}), bf16[16,2,768]{2,1,0:T(2,128)(2,1)S(1)}, u32[]{:S(2)}, u32[]{:S(2)}) async-start(bf16[16,2,768]{2,1,0:T(2,128)(2,1)} %slice.47), calls=%async_computation | async-start | bytes 98304 | tf_op jit(solution)/shard_map/all_to_all | solution.py:45
  129.1 3.3 %collective-permute-start = (bf16[4,3072]{1,0:T(4,128)(2,1)S(1)}, bf16[4,3072]{1,0:T(4,128)(2,1)S(1)}, u32[]{:S(2)}, u32[]{:S(2)}) collective-permute-start(bf16[4,3072]{1,0:T(4,128)(2,1)S(1)} %fusion.20), channel_id=1, source_target_pairs={{0,1},{1,2},{2,3},{3,0},{4,5},{5,6},{6,7},{7,4},{8,9},{9,10},{10,1... | collective-permute-start | bytes 73736 | tf_op jit(solution)/shard_map/ppermute | solution.py:10
